TPU v7x, 256 devices: a whole 4x4x8 slice. The times are simulated.
256 devices in a mesh: lat: 4 (over x_lo, core), lon: 64 (over x_hi, y, z).
Axes of the slice: x: 4 (x_hi: 2, x_lo: 2; x = x_hi * 2 + x_lo), y: 4, z: 8, core: 2. Of those that a mesh axis runs over, the one named last changes fastest.
Arguments:
- field: bfloat16 [512, 2048, 128], P('lat', 'lon'), may hold values from -6 to 6
- land: int32 [512, 2048], P('lat', 'lon'), may hold values 0 or 1
- mirror: int32 [2048], replicated, may hold values from 0 to 2047, as said below
- depth_weight: bfloat16 [49, 128], replicated, may hold values from -2 to 2
- norm_gain: bfloat16 [128], replicated, may hold values from 0.5 to 2
- up_weight: bfloat16 [128, 512], replicated, may hold values from -0.5 to 0.5
- up_bias: bfloat16 [512], replicated, may hold values from -3 to 3
- down_proj: bfloat16 [512, 128], replicated, may hold values from -0.25 to 0.25
- layer_scale: bfloat16 [128], replicated, may hold values from 0.25 to 1
- section_gain: bfloat16 [3, 128], replicated, may hold values from 0.5 to 2
- section_weight: bfloat16 [3, 512, 128], replicated, may hold values from -0.25 to 0.25
- section_bias: bfloat16 [3, 128], replicated, may hold values from -3 to 3
- cotangent: bfloat16 [64, 256, 128], P('lat', 'lon'), may hold values from -6 to 6
Outputs:
- bottleneck: bfloat16 [64, 256, 128], P('lat', 'lon')
- grad_field: bfloat16 [512, 2048, 128], P('lat', 'lon')
- grad_depth: float32 [49, 128], replicated
- grad_up: float32 [128, 512], replicated
- grad_down: float32 [512, 128], replicated
- grad_section: float32 [3, 512, 128], replicated
Inputs may be any that keep to these rules, and one draw needn't show every extreme that they name: mirror[i] = (s - i) mod 2048 for one s, the same for all i; mirror is its own inverse.
All inputs are finite; a program needn't handle non-finite values. No bound on the sum of `land` on one device may be relied on, other than what follows from the above.
Results may differ from a plain program's by a relative error of at most 0.017.
Values may be sent and summed in bfloat16 or wider, within the bound.
A program may use at most 128 MiB of HBM per device.

v0:
```python
import math
import jax
import jax.numpy as jnp
from jax import lax
from jax.sharding import PartitionSpec as P

SECTIONS = 3
epsilon = 1e-06


def extended_2(array, sides, width, wrap):
    for axis, dim in sides:
        peers, length = (lax.axis_size(axis), array.shape[dim])
        up = [(i, (i + 1) % peers) for i in range(peers if wrap else peers - 1)]
        down = [(j, i) for i, j in up]
        last = lax.slice_in_dim(array, length - width, length, axis=dim)
        leading = lax.slice_in_dim(array, 0, width, axis=dim)
        before = lax.ppermute(last, axis, up)
        after = lax.ppermute(leading, axis, down)
        array = jnp.concatenate([before, array, after], axis=dim)
    return array


def norm_parts(values):
    center = values - jnp.mean(values, axis=-1, keepdims=True)
    rstd = lax.rsqrt(jnp.mean(center * center, axis=-1, keepdims=True) + epsilon)
    return (center * rstd, rstd)


def norm_back(grad_hat, normed_hat, rstd):
    first = jnp.mean(grad_hat, axis=-1, keepdims=True)
    second = jnp.mean(grad_hat * normed_hat, axis=-1, keepdims=True)
    return rstd * (grad_hat - first - normed_hat * second)


def gelu_parts(hidden):
    cdf = 0.5 * (1.0 + jax.scipy.special.erf(hidden * 0.7071067811865476))
    dens = jnp.exp(-0.5 * hidden * hidden) * 0.3989422804014327
    return (hidden * cdf, cdf + hidden * dens)


def extend(values):
    widened = extended_2(values, (("lon", 1),), 3, True)
    return extended_2(widened, (("lat", 0),), 3, False)


def on_device(
    field,
    land,
    mirror,
    depth_weight,
    norm_gain,
    up_weight,
    up_bias,
    down_proj,
    layer_scale,
    section_gain,
    section_weight,
    section_bias,
    cotangent,
):
    row_count, col_count, chan_count = field.shape
    lon_count = lax.axis_size("lon")
    total_cols = col_count * lon_count
    total_rows = row_count * lax.axis_size("lat")
    lon_place = lax.axis_index("lon")
    north = lax.axis_index("lat") == lax.axis_size("lat") - 1
    factor = 1.0 / math.sqrt(total_rows * total_cols / 64.0)
    taps = depth_weight.astype(jnp.float32)
    extended = extend(field)
    top_rows = field[row_count - 3 :][::-1]
    every_top = lax.all_gather(top_rows, "lon", axis=1, tiled=True)
    ext_index = jnp.mod(
        lon_place * col_count - 3 + jnp.arange(col_count + 6, dtype=jnp.int32), total_cols
    )
    folded = jnp.take(every_top, jnp.take(mirror, ext_index), axis=1)
    extended = jnp.concatenate(
        [extended[: row_count + 3], jnp.where(north, folded, extended[row_count + 3 :])], axis=0
    )
    depth_out = jnp.zeros((row_count, col_count, chan_count), jnp.float32)
    for tap in range(49):
        tap_row = tap // 7
        tap_col = tap % 7
        depth_out = (
            depth_out
            + extended[tap_row : tap_row + row_count, tap_col : tap_col + col_count].astype(
                jnp.float32
            )
            * taps[tap]
        )
    depth_hat, depth_rstd = norm_parts(depth_out)
    normed = (depth_hat * norm_gain.astype(jnp.float32)).astype(jnp.bfloat16)
    flat = normed.reshape(-1, chan_count)
    hidden = jnp.dot(flat, up_weight, preferred_element_type=jnp.float32) + up_bias.astype(
        jnp.float32
    )
    active_full, slope = gelu_parts(hidden)
    active = active_full.astype(jnp.bfloat16)
    mixed = jnp.dot(active, down_proj, preferred_element_type=jnp.float32).reshape(
        row_count, col_count, chan_count
    )
    land_f = land.astype(jnp.float32)[:, :, None]
    scale_f = layer_scale.astype(jnp.float32)
    level = (land_f * (field.astype(jnp.float32) + scale_f * mixed)).astype(jnp.bfloat16)
    saved = []
    for section in range(SECTIONS):
        section_hat, section_rstd = norm_parts(level.astype(jnp.float32))
        section_norm = (section_hat * section_gain[section].astype(jnp.float32)).astype(
            jnp.bfloat16
        )
        size_r = section_norm.shape[0]
        size_c = section_norm.shape[1]
        patches = section_norm.reshape(size_r // 2, 2, size_c // 2, 2, chan_count)
        kernel = section_weight[section].reshape(2, 2, chan_count, chan_count)
        level = (
            jnp.einsum("iajbc,abcd->ijd", patches, kernel, preferred_element_type=jnp.float32)
            + section_bias[section].astype(jnp.float32)
        ).astype(jnp.bfloat16)
        saved.append((section_hat, section_rstd, patches, kernel))
    upstream = cotangent
    section_list = [None] * SECTIONS
    for section in range(SECTIONS - 1, -1, -1):
        section_hat, section_rstd, patches, kernel = saved[section]
        section_list[section] = jnp.einsum(
            "iajbc,ijd->abcd", patches, upstream, preferred_element_type=jnp.float32
        ).reshape(4 * chan_count, chan_count)
        spread = jnp.einsum(
            "ijd,abcd->iajbc", upstream, kernel, preferred_element_type=jnp.float32
        ).reshape(section_hat.shape)
        upstream = norm_back(
            spread * section_gain[section].astype(jnp.float32), section_hat, section_rstd
        ).astype(jnp.bfloat16)
    section_total = jnp.stack(section_list)
    direct = land_f * upstream.astype(jnp.float32)
    mix_grad = (direct * scale_f).astype(jnp.bfloat16).reshape(-1, chan_count)
    down_sums = jnp.dot(active.T, mix_grad, preferred_element_type=jnp.float32)
    act_grad = jnp.dot(mix_grad, down_proj.T, preferred_element_type=jnp.float32)
    hidden_grad = (act_grad * slope).astype(jnp.bfloat16)
    up_sums = jnp.dot(flat.T, hidden_grad, preferred_element_type=jnp.float32)
    normed_grad = jnp.dot(hidden_grad, up_weight.T, preferred_element_type=jnp.float32).reshape(
        row_count, col_count, chan_count
    )
    depth_grad = norm_back(
        normed_grad * norm_gain.astype(jnp.float32), depth_hat, depth_rstd
    ).astype(jnp.bfloat16)
    depth_f = depth_grad.astype(jnp.float32)
    tap_list = []
    for tap in range(49):
        tap_row = tap // 7
        tap_col = tap % 7
        tap_list.append(
            jnp.sum(
                extended[tap_row : tap_row + row_count, tap_col : tap_col + col_count].astype(
                    jnp.float32
                )
                * depth_f,
                axis=(0, 1),
            )
        )
    tap_sums = jnp.stack(tap_list)
    spread_back = extend(depth_grad)
    padded = jnp.pad(spread_back, ((3, 3), (3, 3), (0, 0)))
    back_sum = jnp.zeros((row_count + 3, col_count, chan_count), jnp.float32)
    for tap in range(49):
        tap_row = tap // 7
        tap_col = tap % 7
        back_sum = (
            back_sum
            + padded[
                9 - tap_row : 12 - tap_row + row_count, 9 - tap_col : 9 - tap_col + col_count
            ].astype(jnp.float32)
            * taps[tap]
        )
    conv_grad = back_sum[:row_count]
    fold_grad = back_sum[row_count:].astype(jnp.bfloat16)
    own_index = lon_place * col_count + jnp.arange(col_count, dtype=jnp.int32)
    targets = jnp.take(mirror, own_index)
    every_grad = lax.all_gather(fold_grad, "lon", axis=1, tiled=True)
    picked = jnp.take(every_grad, targets, axis=1).astype(jnp.float32)
    lower_rows = conv_grad[row_count - 3 :] + jnp.where(north, picked[::-1], 0.0)
    total_grad = direct + jnp.concatenate([conv_grad[: row_count - 3], lower_rows], axis=0)
    grad_field = total_grad.astype(jnp.bfloat16)
    tap_sums, up_sums, down_sums, section_total = lax.psum(
        (tap_sums, up_sums, down_sums, section_total), ("lat", "lon")
    )
    return (
        level,
        grad_field,
        tap_sums * factor,
        up_sums * factor,
        down_sums * factor,
        section_total * factor,
    )


def solution(mesh):
    in_specs = (
        P("lat", "lon", None),
        P("lat", "lon"),
        P(),
        P(),
        P(),
        P(),
        P(),
        P(),
        P(),
        P(),
        P(),
        P(),
        P("lat", "lon", None),
    )
    out_specs = (P("lat", "lon", None), P("lat", "lon", None), P(), P(), P(), P())
    return jax.shard_map(
        on_device, mesh=mesh, in_specs=in_specs, out_specs=out_specs, check_vma=False
    )
```

profile of v0, /device:TPU:8, one launch (start us, length us, event | category | flops | bytes accessed | tf_op | source)
XLA Modules:
  0.0 652.1 jit_solution(4068497093461746249)
XLA Ops:
  8.6 2.0 collective-permute-start
  10.6 3.9 collective-permute-start.1
  33.6 3.2 collective-permute-start.2
  36.8 88.6 %all-gather.3.cloned.1.call-done = bf16[3,2048,128]{2,1,0:T(8,128)(2,1)} async-done(((bf16[3,32,128]{2,1,0:T(8,128)(2,1)}), bf16[3,2048,128]{2,1,0:T(8,128)(2,1)}) %all-gather.3.cloned.1.call-update) | async-done | bytes 1572880 | tf_op jit(solution)/shard_map/all_gather | solution.py:72
  125.3 3.2 copy.132
  130.8 22.6 %fusion.182 = (f32[128,32]{0,1:T(8,128)S(1)}, f32[128,32,128]{2,0,1:T(8,128)S(1)}) fusion(f32[128]{0:T(128)} %get-tuple-element.124, bf16[3,38,128]{2,0,1:T(4,128)(2,1)S(1)} %bitcast_select_fusion, bf16[128,38,128]{2,0,1:T(8,128)(2,1)S(1)} %get-tuple-element.122, f32[128]{0:T(128)} %get-tuple-element.125, f32[128]{0:T(128)} %get-tuple-element.126, ...), kind=kLoop, calls=%fused_computation.493 | loop fusion | flops 143126528 | bytes 10782208 | tf_op jit(solution)/shard_map/reduce_sum | solution.py:25
  156.9 4.6 multiply_convert_fusion
  163.4 4.1 convert_reduce_fusion
  184.4 2.5 multiply_reduce_fusion.2
  188.2 3.5 fusion.12
  195.3 2.1 copy.149
  197.4 2.3 div.71
  199.7 7.5 %multiply_convert_fusion.2 = (bf16[128,32,128]{2,0,1:T(8,128)(2,1)S(1)}, bf16[128,32,128]{2,0,1:T(8,128)(2,1)}) fusion(f32[128]{0:T(128)} %convert_element_type.494, f32[128,32]{0,1:T(8,128)} %convert_element_type.492, f32[128,32]{0,1:T(8,128)} %broadcast_multiply_fusion.12, f32[128,32]{0,1:T(8,128)} %copy-done.36, bf16[128,32,128]{2,0,1:T(8,128)(2,1)} %copy-done.9, ...), kind=kLoop, calls=%fused_computation.273 | loop fusion | flops 6815744 | bytes 5325824 | tf_op jit(solution)/shard_map/convert_element_type | solution.py:135
  207.9 2.0 fusion.192
  209.9 6.9 %fusion.5 = bf16[4096,512]{1,0:T(8,128)(2,1)S(1)} fusion(f32[4096,512]{1,0:T(8,128)} %get-tuple-element.179, bf16[4096,128]{1,0:T(8,128)(2,1)S(1)} %bitcast.315, bf16[512,128]{1,0:T(8,128)(2,1)S(1)} %copy-done.49, f32[512]{0:T(512)S(1)} %copy-done.54), kind=kOutput, calls=%fused_computation.99 | convolution fusion | flops 559939584 | bytes 13764608 | tf_op jit(solution)/shard_map/dot_general | solution.py:137
  218.3 2.6 multiply_reduce_fusion.1
  221.1 3.7 multiply_reduce_fusion
  224.8 7.7 %fusion.113 = (f32[128]{0:T(128)}, f32[128]{0:T(128)}, f32[128]{0:T(128)}, f32[128]{0:T(128)}, f32[128]{0:T(128)}, /*index=5*/f32[128]{0:T(128)}, bf16[128,32,128]{2,0,1:T(8,128)(2,1)S(1)}) fusion(bf16[3,38,128]{2,0,1:T(4,128)(2,1)S(1)} %bitcast_select_fusion, bf16[128,38,128]{2,0,1:T(8,128)(2,1)S(1)} %get-tuple-element.122, ...), kind=kLoop, calls=%fused_computation.262 | loop fusion | flops 23592192 | bytes 6586368 | tf_op jit(solution)/shard_map/reduce_sum | solution.py:152
  232.6 4.1 fusion.114
  247.0 2.6 collective-permute-start.5
  249.6 3.2 fusion.85
  252.9 4.1 fusion.87
  265.6 20.2 %multiply_add_fusion = f32[131,32,128]{2,0,1:T(8,128)S(1)} fusion(bf16[131,38,128]{2,0,1:T(8,128)(2,1)S(1)} %get-tuple-element.102, bf16[134,38,128]{2,0,1:T(8,128)(2,1)S(1)} %pad_maximum_fusion, bf16[131,38,128]{2,0,1:T(8,128)(2,1)S(1)} %get-tuple-element.101, f32[128]{0:T(128)S(1)} %copy-done.79, f32[128]{0:T(128)S(1)} %copy-done.80, ...), kind=kLoop, calls=%fused_computation.159 | loop fusion | flops 78340096 | bytes 34689536 | tf_op jit(solution)/shard_map/add | solution.py:168
  289.2 2.8 fusion.86
  292.0 3.4 fusion.112
  295.7 4.0 fusion.115
  300.1 78.6 %psum.28 = f32[49,128]{1,0:T(8,128)S(1)} all-reduce(f32[49,128]{1,0:T(8,128)S(1)} %stack.202), channel_id=1, replica_groups=mesh['lat'=4,'lon'=64] {'lat','lon'}, use_global_device_ids=true, to_apply=%region_65.66 | all-reduce | flops 6272 | bytes 50176 | tf_op jit(solution)/shard_map/psum | solution.py:183
  379.3 143.9 %all-reduce.4.cloned.1.call-done = (f32[128,512]{1,0:T(8,128)}, f32[512,128]{1,0:T(8,128)}, f32[3,512,128]{2,1,0:T(8,128)}) async-done(((f32[128,512]{1,0:T(8,128)}, f32[512,128]{1,0:T(8,128)}, f32[3,512,128]{2,1,0:T(8,128)}), (f32[128,512]{1,0:T(8,128)}, f32[512,128]{1,0:T(8,128)}, f32[3,512,128]{2,1,0:T(8,128)})) %all-reduce.4.cloned.1.call-update) | async-done | bytes 1310736 | tf_op jit(solution)/shard_map/psum | solution.py:183
  526.6 2.1 broadcast_multiply_fusion
  528.6 105.6 %all-gather.5.cloned.1.call-done = bf16[3,2048,128]{2,1,0:T(8,128)(2,1)} async-done(((bf16[3,32,128]{2,1,0:T(8,128)(2,1)}), bf16[3,2048,128]{2,1,0:T(8,128)(2,1)}) %all-gather.5.cloned.1.call-update) | async-done | bytes 1572880 | tf_op jit(solution)/shard_map/all_gather | solution.py:178
  634.2 4.2 copy.154
  638.4 2.3 gather_fusion.3
  (417 shorter events, 81.8 us)
Async XLA Ops:
  7.2 149.7 %copy-start = (bf16[128,512]{1,0:T(8,128)(2,1)S(1)}, bf16[128,512]{1,0:T(8,128)(2,1)}, u32[]{:S(2)}) copy-start(bf16[128,512]{1,0:T(8,128)(2,1)} %param.18) | copy-start | bytes 393220
  7.2 17.7 %copy-start.12 = (bf16[128,32,128]{2,1,0:T(8,128)(2,1)S(1)}, bf16[128,32,128]{2,1,0:T(8,128)(2,1)}, u32[]{:S(2)}) copy-start(bf16[128,32,128]{2,1,0:T(8,128)(2,1)} %param.13) | copy-start | bytes 3145732
  7.2 12.3 %copy-start.58 = (bf16[49,128]{1,0:T(8,128)(2,1)S(1)}, bf16[49,128]{1,0:T(8,128)(2,1)}, u32[]{:S(2)}) copy-start(bf16[49,128]{1,0:T(8,128)(2,1)} %param.16) | copy-start | bytes 37636
  7.2 12.9 %copy-start.106 = (bf16[3,128]{1,0:T(4,128)(2,1)S(1)}, bf16[3,128]{1,0:T(4,128)(2,1)}, u32[]{:S(2)}) copy-start(bf16[3,128]{1,0:T(4,128)(2,1)} %param.22) | copy-start | bytes 2308
  7.2 13.5 %copy-start.107 = (bf16[3,128]{1,0:T(4,128)(2,1)S(1)}, bf16[3,128]{1,0:T(4,128)(2,1)}, u32[]{:S(2)}) copy-start(bf16[3,128]{1,0:T(4,128)(2,1)} %param.24) | copy-start | bytes 2308
  7.2 16.0 %copy-start.38 = (bf16[3,512,128]{2,1,0:T(8,128)(2,1)S(1)}, bf16[3,512,128]{2,1,0:T(8,128)(2,1)}, u32[]{:S(2)}) copy-start(bf16[3,512,128]{2,1,0:T(8,128)(2,1)} %param.23) | copy-start | bytes 1179652
  7.2 16.7 %copy-start.55 = (bf16[16,4,128]{2,1,0:T(4,128)(2,1)S(1)}, bf16[16,4,128]{2,1,0:T(4,128)(2,1)}, u32[]{:S(2)}) copy-start(bf16[16,4,128]{2,1,0:T(4,128)(2,1)} %param.25) | copy-start | bytes 49156
  7.2 118.1 %all-gather.3.cloned.1.call-start = ((), (), s32[]{:S(2)}) async-start(), calls=%async_computation | async-start | bytes 1597440 | tf_op jit(solution)/shard_map/all_gather | solution.py:72
  8.6 16.2 %collective-permute-start = (bf16[128,3,128]{2,0,1:T(8,128)(2,1)S(1)}, bf16[128,3,128]{2,0,1:T(8,128)(2,1)S(1)}, u32[]{:S(2)}, u32[]{:S(2)}) collective-permute-start(bf16[128,3,128]{2,0,1:T(8,128)(2,1)S(1)} %copy.210), channel_id=1, source_target_pairs={{0,1},{1,2},{2,3},{3,4},{4,5},{5,6},{6,7},{7,8},{8,9},{9,10},{10,1... | collective-permute-start | bytes 294920 | tf_op jit(solution)/shard_map/ppermute | solution.py:18
  10.6 15.1 %collective-permute-start.1 = (bf16[128,3,128]{2,0,1:T(8,128)(2,1)S(1)}, bf16[128,3,128]{2,0,1:T(8,128)(2,1)S(1)}, u32[]{:S(2)}, u32[]{:S(2)}) collective-permute-start(bf16[128,3,128]{2,0,1:T(8,128)(2,1)S(1)} %copy.209), channel_id=1, source_target_pairs={{1,0},{2,1},{3,2},{4,3},{5,4},{6,5},{7,6},{8,7},{9,8},{10,9},{11,1... | collective-permute-start | bytes 294920 | tf_op jit(solution)/shard_map/ppermute | solution.py:19
  15.9 507.3 %all-reduce.4.cloned.1.call-start = ((), (), s32[]{:S(2)}) async-start(), calls=%async_computation.2 | async-start | bytes 2621440 | tf_op jit(solution)/shard_map/psum | solution.py:183
  24.9 5.3 copy-start.140
  24.9 5.9 copy-start.57
  24.9 6.5 copy-start.144
  27.8 102.1 %collective-permute-start.3 = (bf16[3,38,128]{2,0,1:T(4,128)(2,1)S(1)}, bf16[3,38,128]{2,0,1:T(4,128)(2,1)}, u32[]{:S(2)}, u32[]{:S(2)}) collective-permute-start(bf16[3,38,128]{2,0,1:T(4,128)(2,1)S(1)} %get-tuple-element.106), channel_id=1, source_target_pairs={{64,0},{128,64},{192,128},{65,1},{129,65},{193,129},{66,2},{130,66... | collective-permute-start | bytes 87560 | tf_op jit(solution)/shard_map/ppermute | solution.py:19
  33.6 97.3 %collective-permute-start.2 = (bf16[3,38,128]{2,0,1:T(4,128)(2,1)}, bf16[3,38,128]{2,0,1:T(4,128)(2,1)S(1)}, u32[]{:S(2)}, u32[]{:S(2)}) collective-permute-start(bf16[3,38,128]{2,0,1:T(4,128)(2,1)} %get-tuple-element.105), channel_id=1, source_target_pairs={{0,64},{64,128},{128,192},{1,65},{65,129},{129,193},{2,66},{66,130... | collective-permute-start | bytes 87560 | tf_op jit(solution)/shard_map/ppermute | solution.py:18
  153.5 67.6 %copy-start.4 = (f32[128,32,128]{2,0,1:T(8,128)}, f32[128,32,128]{2,0,1:T(8,128)S(1)}, u32[]{:S(2)}) copy-start(f32[128,32,128]{2,0,1:T(8,128)S(1)} %get-tuple-element.100) | copy-start | bytes 6291460
  163.4 5.5 copy-start.63
  199.7 8.2 %copy-start.3 = (bf16[4096,512]{1,0:T(8,128)(2,1)S(1)}, bf16[4096,512]{1,0:T(8,128)(2,1)}, u32[]{:S(2)}) copy-start(bf16[4096,512]{1,0:T(8,128)(2,1)} %copy-done.2) | copy-start | bytes 12582916
  209.9 6.9 %copy-start.17 = (bf16[128,32,128]{2,1,0:T(8,128)(2,1)S(1)}, bf16[128,32,128]{2,1,0:T(8,128)(2,1)}, u32[]{:S(2)}) copy-start(bf16[128,32,128]{2,1,0:T(8,128)(2,1)} %copy-done.16) | copy-start | bytes 3145732
  245.4 11.7 %collective-permute-start.4 = (bf16[128,3,128]{2,0,1:T(8,128)(2,1)S(1)}, bf16[128,3,128]{2,0,1:T(8,128)(2,1)S(1)}, u32[]{:S(2)}, u32[]{:S(2)}) collective-permute-start(bf16[128,3,128]{2,0,1:T(8,128)(2,1)S(1)} %copy-done.51), channel_id=1, source_target_pairs={{0,1},{1,2},{2,3},{3,4},{4,5},{5,6},{6,7},{7,8},{8,9},{9,10},{10,1... | collective-permute-start | bytes 294920 | tf_op jit(solution)/shard_map/ppermute | solution.py:18
  247.0 9.9 %copy-start.56 = (bf16[16,4,128]{2,1,0:T(4,128)(2,1)S(1)}, bf16[16,4,128]{2,1,0:T(4,128)(2,1)}, u32[]{:S(2)}) copy-start(bf16[16,4,128]{2,1,0:T(4,128)(2,1)} %param.25) | copy-start | bytes 49156
  247.0 10.1 %collective-permute-start.5 = (bf16[128,3,128]{2,0,1:T(8,128)(2,1)S(1)}, bf16[128,3,128]{2,0,1:T(8,128)(2,1)S(1)}, u32[]{:S(2)}, u32[]{:S(2)}) collective-permute-start(bf16[128,3,128]{2,0,1:T(8,128)(2,1)S(1)} %copy-done.50), channel_id=1, source_target_pairs={{1,0},{2,1},{3,2},{4,3},{5,4},{6,5},{7,6},{8,7},{9,8},{10,9},{11,1... | collective-permute-start | bytes 294920 | tf_op jit(solution)/shard_map/ppermute | solution.py:19
  252.8 6.9 %copy-start.45 = (f32[1,512,128]{2,1,0:T(8,128)S(1)}, f32[1,512,128]{2,1,0:T(8,128)}, u32[]{:S(2)}) copy-start(f32[1,512,128]{2,1,0:T(8,128)} %convolution_bitcast_fusion.3) | copy-start | bytes 786436
  257.2 3.7 collective-permute-start.6
  258.5 3.9 collective-permute-start.7
  260.8 373.4 %all-gather.5.cloned.1.call-start = ((), (), s32[]{:S(2)}) async-start(), calls=%async_computation.1 | async-start | bytes 1597440 | tf_op jit(solution)/shard_map/all_gather | solution.py:178
  265.6 22.2 %copy-start.27 = (bf16[1,512,128]{2,1,0:T(8,128)(2,1)S(1)}, bf16[1,512,128]{2,1,0:T(8,128)(2,1)}, u32[]{:S(2)}) copy-start(bf16[1,512,128]{2,1,0:T(8,128)(2,1)} %copy-done.26) | copy-start | bytes 393220
  289.2 6.2 copy-start.14
  528.6 112.1 %copy-start.141 = (pred[32]{0:T(512)(128)(4,1)S(1)}, pred[32]{0:T(512)(128)(4,1)}, u32[]{:S(2)}) copy-start(pred[32]{0:T(512)(128)(4,1)} %compare_and_fusion) | copy-start | bytes 100
  528.6 113.2 %slice-start = ((f32[131,32,128]{2,0,1:T(8,128)}), f32[125,32,128]{2,0,1:T(8,128)S(1)}, s32[]{:S(2)}) async-start(f32[131,32,128]{2,0,1:T(8,128)} %copy-done.18), calls=%async_computation.3 | async-start | bytes 4194304 | tf_op jit(solution)/shard_map/slice | solution.py:181
  528.6 113.2 %copy-start.40 = (f32[128,32]{0,1:T(8,128)S(1)}, f32[128,32]{0,1:T(8,128)}, u32[]{:S(2)}) copy-start(f32[128,32]{0,1:T(8,128)} %convert_element_type.492) | copy-start | bytes 49156
  (125 other events, 361.2 us)
Sparse Core Ops, SparseCore 0:
  16.0 109.2 all-gather.2
  260.9 262.2 all-reduce.3
  526.7 107.4 all-gather.4
where the time goes:
time: 657 us; the launch traced here: 652 us
  waiting for transfers between devices  340 us (52%)
  other arithmetic  125 us (19%)
  blocking collectives  78.6 us (12%)
  local copies, waits for them, and re-layouts  47.4 us (7%)
  matrix products  27.5 us (4%)
  starting transfers between devices  17.3 us (3%)
  between operations  16.4 us (2%)
    psum x1, waiting for transfers between devices, on_device(): lax.psum((tap_sums, up_sums, down_sums, section_total), ('lat', 'lon'))  144 us
    all_gather x1, waiting for transfers between devices, on_device(): every_grad = lax.all_gather(fold_grad, 'lon', axis=1, tiled=True)  106 us
    all_gather x1, waiting for transfers between devices, on_device(): every_top = lax.all_gather(top_rows, 'lon', axis=1, tiled=True)  88.6 us
    psum x1, blocking collectives, on_device(): lax.psum((tap_sums, up_sums, down_sums, section_total), ('lat', 'lon'))  78.6 us
    reduce_sum x8, other arithmetic, on_device(): jnp.sum(extended[tap_row:tap_row + row_count, tap_col:tap_col + col_count...  31.3 us
    reduce_sum x2, other arithmetic, norm_parts(): center = values - jnp.mean(values, axis=-1, keepdims=True)  26.7 us
    add x1, other arithmetic, on_device(): back_sum + padded[9 - tap_row:12 - tap_row + row_count, 9 - tap_col:9 - t...  20.2 us
  transfers between devices with their start and end apart: 11, of which 4 were waited for; matrix products, arithmetic and copies ran while one was open for 11% of the time, Pallas kernels for 0%

commit v1 on v0

--- a/solution.py
+++ b/solution.py
@@ -175,7 +175,9 @@
     fold_grad = back_sum[row_count:].astype(jnp.bfloat16)
     own_index = lon_place * col_count + jnp.arange(col_count, dtype=jnp.int32)
     targets = jnp.take(mirror, own_index)
-    every_grad = lax.all_gather(fold_grad, "lon", axis=1, tiled=True)
+    every_grad = jnp.concatenate(
+        lax.all_to_all(jnp.stack([fold_grad] * lax.axis_size("lon")), "lon", 0, 0), axis=1
+    )
     picked = jnp.take(every_grad, targets, axis=1).astype(jnp.float32)
     lower_rows = conv_grad[row_count - 3 :] + jnp.where(north, picked[::-1], 0.0)
     total_grad = direct + jnp.concatenate([conv_grad[: row_count - 3], lower_rows], axis=0)

time: 657 us -> 547 us (0.83)
  waiting for transfers between devices: 340 us -> 208 us
  local copies, waits for them, and re-layouts: 47.4 us -> 58.1 us
  starting transfers between devices: 17.3 us -> 27.3 us
    all_gather x1 -> x0, waiting for transfers between devices: 106 us -> none  [on_device(): every_grad = lax.all_gather(fold_grad, 'lon', axis=1, tiled=True)]
    psum x1, waiting for transfers between devices: 144 us -> 118 us  [on_device(): lax.psum((tap_sums, up_sums, down_sums, section_total), ('lat', 'lon'))]
    reshape x0 -> x1, local copies, waits for them, and re-layouts: none -> 10.7 us  [on_device(): jnp.concatenate(lax.all_to_all(jnp.stack([fold_grad] * lax.axis_size('lon...]
    all_to_all x0 -> x1, starting transfers between devices: none -> 9.85 us  [on_device(): lax.all_to_all(jnp.stack([fold_grad] * lax.axis_size('lon')), 'lon', 0, 0)]
  transfers between devices with their start and end apart: 11 -> 11, of which waited for: 4 -> 3; matrix products, arithmetic and copies ran while one was open for 11% -> 14% of each run, Pallas kernels for 0% -> 0%
where the time goes in v1:
time: 547 us; the launch traced here: 542 us
  waiting for transfers between devices  208 us (38%)
  other arithmetic  123 us (22%)
  blocking collectives  80.8 us (15%)
  local copies, waits for them, and re-layouts  58.1 us (11%)
  matrix products  27.6 us (5%)
  starting transfers between devices  27.3 us (5%)
  between operations  16.5 us (3%)
    psum x1, waiting for transfers between devices, on_device(): lax.psum((tap_sums, up_sums, down_sums, section_total), ('lat', 'lon'))  118 us
    all_gather x1, waiting for transfers between devices, on_device(): every_top = lax.all_gather(top_rows, 'lon', axis=1, tiled=True)  88.6 us
    psum x1, blocking collectives, on_device(): lax.psum((tap_sums, up_sums, down_sums, section_total), ('lat', 'lon'))  80.8 us
    reduce_sum x8, other arithmetic, on_device(): jnp.sum(extended[tap_row:tap_row + row_count, tap_col:tap_col + col_count...  29.3 us
    reduce_sum x2, other arithmetic, norm_parts(): center = values - jnp.mean(values, axis=-1, keepdims=True)  26.7 us
    add x1, other arithmetic, on_device(): back_sum + padded[9 - tap_row:12 - tap_row + row_count, 9 - tap_col:9 - t...  20.5 us
  transfers between devices with their start and end apart: 11, of which 3 were waited for; matrix products, arithmetic and copies ran while one was open for 14% of the time, Pallas kernels for 0%

profile of v1, /device:TPU:8, one launch (start us, length us, event | category | flops | bytes accessed | tf_op | source)
XLA Modules:
  0.0 541.9 jit_solution(9116973558509474068)
XLA Ops:
  8.6 2.0 collective-permute-start
  10.6 3.9 collective-permute-start.1
  33.6 3.2 collective-permute-start.2
  36.8 88.6 %all-gather.2.cloned.1.call-done = bf16[3,2048,128]{2,1,0:T(8,128)(2,1)} async-done(((bf16[3,32,128]{2,1,0:T(8,128)(2,1)}), bf16[3,2048,128]{2,1,0:T(8,128)(2,1)}) %all-gather.2.cloned.1.call-update) | async-done | bytes 1572880 | tf_op jit(solution)/shard_map/all_gather | solution.py:72
  125.3 3.2 copy.137
  130.8 22.6 %fusion.182 = (f32[128,32]{0,1:T(8,128)S(1)}, f32[128,32,128]{2,0,1:T(8,128)S(1)}) fusion(f32[128]{0:T(128)} %get-tuple-element.124, bf16[3,38,128]{2,0,1:T(4,128)(2,1)S(1)} %bitcast_select_fusion, bf16[128,38,128]{2,0,1:T(8,128)(2,1)S(1)} %get-tuple-element.122, f32[128]{0:T(128)} %get-tuple-element.125, f32[128]{0:T(128)} %get-tuple-element.126, ...), kind=kLoop, calls=%fused_computation.493 | loop fusion | flops 143126528 | bytes 10782208 | tf_op jit(solution)/shard_map/reduce_sum | solution.py:25
  156.9 4.6 multiply_convert_fusion
  163.4 4.1 convert_reduce_fusion
  184.4 2.5 multiply_reduce_fusion.2
  188.2 3.5 fusion.12
  195.3 2.1 copy.154
  197.4 2.3 div.71
  199.7 7.5 %multiply_convert_fusion.2 = (bf16[128,32,128]{2,0,1:T(8,128)(2,1)S(1)}, bf16[128,32,128]{2,0,1:T(8,128)(2,1)}) fusion(f32[128]{0:T(128)} %convert_element_type.494, f32[128,32]{0,1:T(8,128)} %convert_element_type.492, f32[128,32]{0,1:T(8,128)} %broadcast_multiply_fusion.12, f32[128,32]{0,1:T(8,128)} %copy-done.37, bf16[128,32,128]{2,0,1:T(8,128)(2,1)} %copy-done.9, ...), kind=kLoop, calls=%fused_computation.273 | loop fusion | flops 6815744 | bytes 5325824 | tf_op jit(solution)/shard_map/convert_element_type | solution.py:135
  207.9 2.0 fusion.192
  209.9 6.9 %fusion.5 = bf16[4096,512]{1,0:T(8,128)(2,1)S(1)} fusion(f32[4096,512]{1,0:T(8,128)} %get-tuple-element.179, bf16[4096,128]{1,0:T(8,128)(2,1)S(1)} %bitcast.319, bf16[512,128]{1,0:T(8,128)(2,1)S(1)} %copy-done.49, f32[512]{0:T(512)S(1)} %copy-done.54), kind=kOutput, calls=%fused_computation.99 | convolution fusion | flops 559939584 | bytes 13764608 | tf_op jit(solution)/shard_map/dot_general | solution.py:137
  218.3 2.6 multiply_reduce_fusion.1
  221.1 3.7 multiply_reduce_fusion
  224.8 7.7 %fusion.113 = (f32[128]{0:T(128)}, f32[128]{0:T(128)}, f32[128]{0:T(128)}, f32[128]{0:T(128)}, f32[128]{0:T(128)}, /*index=5*/f32[128]{0:T(128)}, bf16[128,32,128]{2,0,1:T(8,128)(2,1)S(1)}) fusion(bf16[3,38,128]{2,0,1:T(4,128)(2,1)S(1)} %bitcast_select_fusion, bf16[128,38,128]{2,0,1:T(8,128)(2,1)S(1)} %get-tuple-element.122, ...), kind=kLoop, calls=%fused_computation.262 | loop fusion | flops 23592192 | bytes 6586368 | tf_op jit(solution)/shard_map/reduce_sum | solution.py:152
  232.6 4.1 fusion.114
  246.0 2.6 collective-permute-start.5
  250.4 2.5 fusion.85
  253.0 2.8 fusion.86
  264.2 20.5 %multiply_add_fusion = f32[131,32,128]{2,0,1:T(8,128)S(1)} fusion(bf16[131,38,128]{2,0,1:T(8,128)(2,1)S(1)} %get-tuple-element.102, bf16[134,38,128]{2,0,1:T(8,128)(2,1)S(1)} %pad_maximum_fusion, bf16[131,38,128]{2,0,1:T(8,128)(2,1)S(1)} %get-tuple-element.101, f32[128]{0:T(128)S(1)} %copy-done.78, f32[128]{0:T(128)S(1)} %copy-done.79, ...), kind=kLoop, calls=%fused_computation.159 | loop fusion | flops 78340096 | bytes 34689536 | tf_op jit(solution)/shard_map/add | solution.py:168
  287.5 9.8 %all-to-all-start = ((bf16[64,3,32,128]{3,2,1,0:T(8,128)(2,1)}), bf16[64,3,32,128]{3,2,1,0:T(8,128)(2,1)}, u32[]{:S(2)}, u32[]{:S(2)}) async-start(bf16[64,3,32,128]{3,2,1,0:T(8,128)(2,1)} %stack.104), calls=%async_computation | async-start | bytes 3145728 | tf_op jit(solution)/shard_map/all_to_all | solution.py:179
  297.4 3.5 fusion.87
  300.8 3.4 fusion.112
  304.2 4.0 fusion.115
  310.1 80.8 %psum.28 = f32[49,128]{1,0:T(8,128)S(1)} all-reduce(f32[49,128]{1,0:T(8,128)S(1)} %stack.270), channel_id=1, replica_groups=mesh['lat'=4,'lon'=64] {'lat','lon'}, use_global_device_ids=true, to_apply=%region_65.66 | all-reduce | flops 6272 | bytes 50176 | tf_op jit(solution)/shard_map/psum | solution.py:185
  393.2 117.9 %all-reduce.4.cloned.1.call-done = (f32[128,512]{1,0:T(8,128)}, f32[512,128]{1,0:T(8,128)}, f32[3,512,128]{2,1,0:T(8,128)}) async-done(((f32[128,512]{1,0:T(8,128)}, f32[512,128]{1,0:T(8,128)}, f32[3,512,128]{2,1,0:T(8,128)}), (f32[128,512]{1,0:T(8,128)}, f32[512,128]{1,0:T(8,128)}, f32[3,512,128]{2,1,0:T(8,128)})) %all-reduce.4.cloned.1.call-update) | async-done | bytes 1310736 | tf_op jit(solution)/shard_map/psum | solution.py:185
  514.4 2.1 broadcast_multiply_fusion
  518.2 10.7 %copy.160 = bf16[3,2048,128]{2,0,1:T(4,128)(2,1)} copy(bf16[3,2048,128]{2,1,0:T(8,128)(2,1)S(1)} %bitcast.313) | data formatting | bytes 3145728 | tf_op jit(solution)/shard_map/reshape | solution.py:178
  529.0 2.3 gather_fusion.3
  (383 shorter events, 85.5 us)
Async XLA Ops:
  7.2 149.7 %copy-start = (bf16[128,512]{1,0:T(8,128)(2,1)S(1)}, bf16[128,512]{1,0:T(8,128)(2,1)}, u32[]{:S(2)}) copy-start(bf16[128,512]{1,0:T(8,128)(2,1)} %param.18) | copy-start | bytes 393220
  7.2 17.7 %copy-start.12 = (bf16[128,32,128]{2,1,0:T(8,128)(2,1)S(1)}, bf16[128,32,128]{2,1,0:T(8,128)(2,1)}, u32[]{:S(2)}) copy-start(bf16[128,32,128]{2,1,0:T(8,128)(2,1)} %param.13) | copy-start | bytes 3145732
  7.2 12.3 %copy-start.57 = (bf16[49,128]{1,0:T(8,128)(2,1)S(1)}, bf16[49,128]{1,0:T(8,128)(2,1)}, u32[]{:S(2)}) copy-start(bf16[49,128]{1,0:T(8,128)(2,1)} %param.16) | copy-start | bytes 37636
  7.2 12.9 %copy-start.106 = (bf16[3,128]{1,0:T(4,128)(2,1)S(1)}, bf16[3,128]{1,0:T(4,128)(2,1)}, u32[]{:S(2)}) copy-start(bf16[3,128]{1,0:T(4,128)(2,1)} %param.22) | copy-start | bytes 2308
  7.2 13.5 %copy-start.107 = (bf16[3,128]{1,0:T(4,128)(2,1)S(1)}, bf16[3,128]{1,0:T(4,128)(2,1)}, u32[]{:S(2)}) copy-start(bf16[3,128]{1,0:T(4,128)(2,1)} %param.24) | copy-start | bytes 2308
  7.2 15.9 %copy-start.39 = (bf16[3,512,128]{2,1,0:T(8,128)(2,1)S(1)}, bf16[3,512,128]{2,1,0:T(8,128)(2,1)}, u32[]{:S(2)}) copy-start(bf16[3,512,128]{2,1,0:T(8,128)(2,1)} %param.23) | copy-start | bytes 1179652
  7.2 16.7 %copy-start.55 = (bf16[16,4,128]{2,1,0:T(4,128)(2,1)S(1)}, bf16[16,4,128]{2,1,0:T(4,128)(2,1)}, u32[]{:S(2)}) copy-start(bf16[16,4,128]{2,1,0:T(4,128)(2,1)} %param.25) | copy-start | bytes 49156
  7.2 118.1 %all-gather.2.cloned.1.call-start = ((), (), s32[]{:S(2)}) async-start(), calls=%async_computation.1 | async-start | bytes 1597440 | tf_op jit(solution)/shard_map/all_gather | solution.py:72
  8.6 16.2 %collective-permute-start = (bf16[128,3,128]{2,0,1:T(8,128)(2,1)S(1)}, bf16[128,3,128]{2,0,1:T(8,128)(2,1)S(1)}, u32[]{:S(2)}, u32[]{:S(2)}) collective-permute-start(bf16[128,3,128]{2,0,1:T(8,128)(2,1)S(1)} %copy.216), channel_id=1, source_target_pairs={{0,1},{1,2},{2,3},{3,4},{4,5},{5,6},{6,7},{7,8},{8,9},{9,10},{10,1... | collective-permute-start | bytes 294920 | tf_op jit(solution)/shard_map/ppermute | solution.py:18
  10.6 15.1 %collective-permute-start.1 = (bf16[128,3,128]{2,0,1:T(8,128)(2,1)S(1)}, bf16[128,3,128]{2,0,1:T(8,128)(2,1)S(1)}, u32[]{:S(2)}, u32[]{:S(2)}) collective-permute-start(bf16[128,3,128]{2,0,1:T(8,128)(2,1)S(1)} %copy.215), channel_id=1, source_target_pairs={{1,0},{2,1},{3,2},{4,3},{5,4},{6,5},{7,6},{8,7},{9,8},{10,9},{11,1... | collective-permute-start | bytes 294920 | tf_op jit(solution)/shard_map/ppermute | solution.py:19
  15.9 495.2 %all-reduce.4.cloned.1.call-start = ((), (), s32[]{:S(2)}) async-start(), calls=%async_computation.2 | async-start | bytes 2621440 | tf_op jit(solution)/shard_map/psum | solution.py:185
  24.9 5.3 copy-start.123
  24.9 5.9 %copy-start.56 = (s32[128,32]{0,1:T(8,128)S(1)}, s32[128,32]{0,1:T(8,128)}, u32[]{:S(2)}) copy-start(s32[128,32]{0,1:T(8,128)} %param.14) | copy-start | bytes 49156
  24.9 6.5 %copy-start.127 = (bf16[128]{0:T(256)(128)(2,1)S(1)}, bf16[128]{0:T(256)(128)(2,1)}, u32[]{:S(2)}) copy-start(bf16[128]{0:T(256)(128)(2,1)} %param.21) | copy-start | bytes 772
  27.8 102.1 %collective-permute-start.3 = (bf16[3,38,128]{2,0,1:T(4,128)(2,1)S(1)}, bf16[3,38,128]{2,0,1:T(4,128)(2,1)}, u32[]{:S(2)}, u32[]{:S(2)}) collective-permute-start(bf16[3,38,128]{2,0,1:T(4,128)(2,1)S(1)} %get-tuple-element.106), channel_id=1, source_target_pairs={{64,0},{128,64},{192,128},{65,1},{129,65},{193,129},{66,2},{130,66... | collective-permute-start | bytes 87560 | tf_op jit(solution)/shard_map/ppermute | solution.py:19
  33.6 97.3 %collective-permute-start.2 = (bf16[3,38,128]{2,0,1:T(4,128)(2,1)}, bf16[3,38,128]{2,0,1:T(4,128)(2,1)S(1)}, u32[]{:S(2)}, u32[]{:S(2)}) collective-permute-start(bf16[3,38,128]{2,0,1:T(4,128)(2,1)} %get-tuple-element.105), channel_id=1, source_target_pairs={{0,64},{64,128},{128,192},{1,65},{65,129},{129,193},{2,66},{66,130... | collective-permute-start | bytes 87560 | tf_op jit(solution)/shard_map/ppermute | solution.py:18
  153.5 67.6 %copy-start.4 = (f32[128,32,128]{2,0,1:T(8,128)}, f32[128,32,128]{2,0,1:T(8,128)S(1)}, u32[]{:S(2)}) copy-start(f32[128,32,128]{2,0,1:T(8,128)S(1)} %get-tuple-element.100) | copy-start | bytes 6291460
  163.4 5.5 %copy-start.62 = (f32[128]{0:T(128)S(1)}, f32[128]{0:T(128)}, u32[]{:S(2)}) copy-start(f32[128]{0:T(128)} %get-tuple-element.176) | copy-start | bytes 1540
  199.7 8.2 %copy-start.3 = (bf16[4096,512]{1,0:T(8,128)(2,1)S(1)}, bf16[4096,512]{1,0:T(8,128)(2,1)}, u32[]{:S(2)}) copy-start(bf16[4096,512]{1,0:T(8,128)(2,1)} %copy-done.2) | copy-start | bytes 12582916
  209.9 6.9 %copy-start.17 = (bf16[128,32,128]{2,1,0:T(8,128)(2,1)S(1)}, bf16[128,32,128]{2,1,0:T(8,128)(2,1)}, u32[]{:S(2)}) copy-start(bf16[128,32,128]{2,1,0:T(8,128)(2,1)} %copy-done.16) | copy-start | bytes 3145732
  240.2 5.7 %copy-start.50 = (bf16[128,3,128]{2,0,1:T(8,128)(2,1)S(1)}, bf16[128,3,128]{2,0,1:T(8,128)(2,1)}, u32[]{:S(2)}) copy-start(bf16[128,3,128]{2,0,1:T(8,128)(2,1)} %get-tuple-element.108) | copy-start | bytes 294916
  244.3 11.4 %collective-permute-start.4 = (bf16[128,3,128]{2,0,1:T(8,128)(2,1)S(1)}, bf16[128,3,128]{2,0,1:T(8,128)(2,1)S(1)}, u32[]{:S(2)}, u32[]{:S(2)}) collective-permute-start(bf16[128,3,128]{2,0,1:T(8,128)(2,1)S(1)} %copy-done.51), channel_id=1, source_target_pairs={{0,1},{1,2},{2,3},{3,4},{4,5},{5,6},{6,7},{7,8},{8,9},{9,10},{10,1... | collective-permute-start | bytes 294920 | tf_op jit(solution)/shard_map/ppermute | solution.py:18
  246.0 9.8 %collective-permute-start.5 = (bf16[128,3,128]{2,0,1:T(8,128)(2,1)S(1)}, bf16[128,3,128]{2,0,1:T(8,128)(2,1)S(1)}, u32[]{:S(2)}, u32[]{:S(2)}) collective-permute-start(bf16[128,3,128]{2,0,1:T(8,128)(2,1)S(1)} %copy-done.50), channel_id=1, source_target_pairs={{1,0},{2,1},{3,2},{4,3},{5,4},{6,5},{7,6},{8,7},{9,8},{10,9},{11,1... | collective-permute-start | bytes 294920 | tf_op jit(solution)/shard_map/ppermute | solution.py:19
  252.9 5.7 %copy-start.28 = (bf16[1,512,128]{2,1,0:T(8,128)(2,1)S(1)}, bf16[1,512,128]{2,1,0:T(8,128)(2,1)}, u32[]{:S(2)}) copy-start(bf16[1,512,128]{2,1,0:T(8,128)(2,1)} %copy-done.27) | copy-start | bytes 393220
  253.0 5.7 %copy-start.115 = (f32[128]{0:T(128)S(1)}, f32[128]{0:T(128)}, u32[]{:S(2)}) copy-start(f32[128]{0:T(128)} %get-tuple-element.172) | copy-start | bytes 1540
  255.8 3.6 collective-permute-start.6
  257.1 3.9 collective-permute-start.7
  287.5 229.0 %all-to-all-start = ((bf16[64,3,32,128]{3,2,1,0:T(8,128)(2,1)}), bf16[64,3,32,128]{3,2,1,0:T(8,128)(2,1)}, u32[]{:S(2)}, u32[]{:S(2)}) async-start(bf16[64,3,32,128]{3,2,1,0:T(8,128)(2,1)} %stack.104), calls=%async_computation | async-start | bytes 3145728 | tf_op jit(solution)/shard_map/all_to_all | solution.py:179
  297.3 6.9 %copy-start.14 = (bf16[128,32,128]{2,1,0:T(8,128)(2,1)S(1)}, bf16[128,32,128]{2,1,0:T(8,128)(2,1)}, u32[]{:S(2)}) copy-start(bf16[128,32,128]{2,1,0:T(8,128)(2,1)} %param.13) | copy-start | bytes 3145732
  518.2 13.1 %copy-start.124 = (pred[32]{0:T(512)(128)(4,1)S(1)}, pred[32]{0:T(512)(128)(4,1)}, u32[]{:S(2)}) copy-start(pred[32]{0:T(512)(128)(4,1)} %compare_and_fusion) | copy-start | bytes 100
  518.2 14.2 %copy-start.23 = (bf16[128,32,128]{2,0,1:T(8,128)(2,1)S(1)}, bf16[128,32,128]{2,0,1:T(8,128)(2,1)}, u32[]{:S(2)}) copy-start(bf16[128,32,128]{2,0,1:T(8,128)(2,1)} %get-tuple-element.96) | copy-start | bytes 3145732
  518.2 14.2 %copy-start.41 = (f32[128,32]{0,1:T(8,128)S(1)}, f32[128,32]{0,1:T(8,128)}, u32[]{:S(2)}) copy-start(f32[128,32]{0,1:T(8,128)} %convert_element_type.492) | copy-start | bytes 49156
  (107 other events, 249.2 us)
Sparse Core Ops, SparseCore 0:
  16.0 109.2 all-gather.1
  250.6 260.4 all-reduce.3
